TPU v7x, 512 devices: a whole 4x4x16 slice. The times are simulated.
512 devices in a mesh: context: 32 (over x, y, z_hi), tensor: 16 (over z_lo, core).
Axes of the slice: x: 4, y: 4, z: 16 (z_hi: 2, z_lo: 8; z = z_hi * 8 + z_lo), core: 2. Of those that a mesh axis runs over, the one named last changes fastest.
Arguments:
- inputs: float32 [128, 131072], P('tensor', 'context'), may hold values from -0.0390625 to 0.0390625
- grads: float32 [128, 131072], P('tensor', 'context'), may hold values from -6 to 6
- response: float32 [128, 131072], P('tensor', 'context'), may hold values from -0.0390625 to 0.0390625
Outputs:
- input_grad: float32 [128, 131072], P('tensor', 'context')
- filter_grad: float32 [128, 131072], P('tensor', 'context')
All inputs are finite; a program needn't handle non-finite values.
Results may differ from a plain program's by a relative error of at most 0.00014.
Values sent between devices are 32-bit elements; how exact they have to be, the bound alone decides.
A program may use at most 64 MiB of HBM per device.

v0:
```python
import math

import jax
import jax.numpy as jnp
from jax import lax
from jax.sharding import PartitionSpec as P

RADIX = 128


HIGHEST = lax.Precision.HIGHEST


def phase_pair(row_index, col_index, period, sign_flip):
    product = row_index[:, None] * col_index[None, :] % period
    angles = 2.0 * math.pi / period * product.astype(jnp.float32)
    return (jnp.cos(angles), sign_flip * jnp.sin(angles))


def complex_apply(pattern, tables, values):
    real_real = jnp.einsum(pattern, tables[0], values[0], precision=HIGHEST)
    imag_imag = jnp.einsum(pattern, tables[1], values[1], precision=HIGHEST)
    real_imag = jnp.einsum(pattern, tables[0], values[1], precision=HIGHEST)
    imag_real = jnp.einsum(pattern, tables[1], values[0], precision=HIGHEST)
    return (real_real - imag_imag, real_imag + imag_real)


def complex_times(left_pair, right_pair):
    return (
        left_pair[0] * right_pair[0] - left_pair[1] * right_pair[1],
        left_pair[0] * right_pair[1] + left_pair[1] * right_pair[0],
    )


def per_device(inputs, grads, response):
    context_size = lax.axis_size("context")
    device_index = lax.axis_index("context")
    channels, block_len = inputs.shape
    column_len = block_len // context_size
    full_length = block_len * context_size
    padded_len = 2 * full_length
    split_len = block_len // RADIX
    freq_rows = jnp.arange(2 * context_size, dtype=jnp.int32)
    part_rows = jnp.arange(context_size, dtype=jnp.int32)
    outer_fwd = phase_pair(freq_rows, part_rows, 2 * context_size, -1.0)
    outer_inv = phase_pair(part_rows, freq_rows, 2 * context_size, 1.0)
    split_rows = jnp.arange(split_len, dtype=jnp.int32)
    radix_rows = jnp.arange(RADIX, dtype=jnp.int32)
    first_fwd = phase_pair(split_rows, split_rows, split_len, -1.0)
    first_inv = (first_fwd[0], -first_fwd[1])
    inner_fwd = phase_pair(split_rows, radix_rows, block_len, -1.0)
    inner_inv = (inner_fwd[0], -inner_fwd[1])
    last_fwd = phase_pair(radix_rows, radix_rows, RADIX, -1.0)
    last_inv = (last_fwd[0], -last_fwd[1])
    pair_rows = 2 * device_index + jnp.arange(2, dtype=jnp.int32)
    column_rows = jnp.arange(block_len, dtype=jnp.int32)
    global_fwd = phase_pair(pair_rows, column_rows, padded_len, -1.0)
    global_inv = (global_fwd[0], -global_fwd[1])
    signals = jnp.stack([inputs, grads, response])
    columns = lax.all_to_all(
        signals.reshape(3, channels, context_size, column_len),
        "context",
        split_axis=2,
        concat_axis=2,
        tiled=True,
    )
    real_part = jnp.einsum("kn,smnj->smkj", outer_fwd[0], columns, precision=HIGHEST)
    imag_part = jnp.einsum("kn,smnj->smkj", outer_fwd[1], columns, precision=HIGHEST)
    columns = jnp.stack([real_part, imag_part], axis=1)
    arrived = lax.all_to_all(columns, "context", split_axis=3, concat_axis=4, tiled=True)
    values = complex_times((arrived[:, 0], arrived[:, 1]), global_fwd)
    shaped = tuple((v.reshape(v.shape[:3] + (split_len, RADIX)) for v in values))
    sectioned = complex_apply("xa,smrab->smrxb", first_fwd, shaped)
    turned = complex_times(sectioned, inner_fwd)
    spec_real, spec_imag = complex_apply("bd,smrxb->smrxd", last_fwd, turned)
    back_input = (
        spec_real[2] * spec_real[1] + spec_imag[2] * spec_imag[1],
        spec_real[2] * spec_imag[1] - spec_imag[2] * spec_real[1],
    )
    back_filter = (
        spec_real[0] * spec_real[1] + spec_imag[0] * spec_imag[1],
        spec_real[0] * spec_imag[1] - spec_imag[0] * spec_real[1],
    )
    inverse_in = ((back_input[0] - back_filter[1])[None], (back_input[1] + back_filter[0])[None])
    sectioned = complex_apply("bd,smrxd->smrxb", last_inv, inverse_in)
    turned = complex_times(sectioned, inner_inv)
    rebuilt = complex_apply("ax,smrxb->smrab", first_inv, turned)
    flat = tuple((v.reshape(v.shape[:3] + (block_len,)) for v in rebuilt))
    untwisted = complex_times(flat, global_inv)
    rows_back = jnp.stack([untwisted[0], untwisted[1]], axis=1)
    arrived = lax.all_to_all(rows_back, "context", split_axis=4, concat_axis=3, tiled=True)
    cos_real = jnp.einsum("nk,smkj->smnj", outer_inv[0], arrived[:, 0], precision=HIGHEST)
    sin_imag = jnp.einsum("nk,smkj->smnj", outer_inv[1], arrived[:, 1], precision=HIGHEST)
    cos_imag = jnp.einsum("nk,smkj->smnj", outer_inv[0], arrived[:, 1], precision=HIGHEST)
    sin_real = jnp.einsum("nk,smkj->smnj", outer_inv[1], arrived[:, 0], precision=HIGHEST)
    folded = jnp.concatenate([cos_real - sin_imag, cos_imag + sin_real], axis=0) / padded_len
    restored = lax.all_to_all(folded, "context", split_axis=2, concat_axis=3, tiled=True).reshape(
        2, channels, block_len
    )
    return (restored[0], restored[1])


def solution(mesh):
    return jax.shard_map(
        per_device,
        mesh=mesh,
        in_specs=(P("tensor", "context"), P("tensor", "context"), P("tensor", "context")),
        out_specs=(P("tensor", "context"), P("tensor", "context")),
        check_vma=False,
    )
```

profile of v0, /device:TPU:32, one launch (start us, length us, event | category | flops | bytes accessed | tf_op | source)
XLA Modules:
  0.0 262.2 jit_solution(6345385998598428657)
XLA Ops:
  0.6 1.1 pad_maximum_fusion.2
  1.7 51.7 %all_to_all.50 = f32[3,8,32,128]{3,1,0,2:T(8,128)S(1)} all-to-all(f32[3,8,32,128]{3,1,0,2:T(8,128)S(1)} %pad_maximum_fusion.2), channel_id=1, replica_groups=mesh['context'=32,'tensor'=16] {'context'}, dimensions={2} | all-to-all | bytes 786432 | tf_op jit(solution)/shard_map/all_to_all | solution.py:60
  53.4 0.9 convolution_bitcast_fusion
  54.3 0.9 convolution_bitcast_fusion.1
  55.4 2.1 copy.31
  57.5 4.1 %all-to-all-start.1 = ((f32[3,2,8,64,128]{4,2,0,1,3:T(8,128)}), f32[3,2,8,64,128]{4,2,0,1,3:T(8,128)S(1)}, u32[]{:S(2)}, u32[]{:S(2)}) async-start(f32[3,2,8,64,128]{4,2,0,1,3:T(8,128)} %copy.31), calls=%async_computation.1 | async-start | bytes 3145728 | tf_op jit(solution)/shard_map/all_to_all | solution.py:70
  62.1 0.6 fusion.85
  62.7 69.5 %all-to-all-done.1 = f32[3,2,8,64,128]{4,2,0,1,3:T(8,128)S(1)} async-done(((f32[3,2,8,64,128]{4,2,0,1,3:T(8,128)}), f32[3,2,8,64,128]{4,2,0,1,3:T(8,128)S(1)}, u32[]{:S(2)}, u32[]{:S(2)}) %all-to-all-start.1) | async-done | bytes 1572896 | tf_op jit(solution)/shard_map/all_to_all | solution.py:70
  132.2 0.9 copy.75
  133.5 1.1 fusion.18
  134.6 1.1 fusion.19
  135.7 1.1 fusion.1
  136.8 1.1 fusion
  138.0 1.0 fusion.16
  139.0 1.0 fusion.17
  140.0 1.0 convolution_subtract_fusion
  141.1 1.0 convolution_add_fusion
  142.3 0.6 fusion.12
  142.9 0.8 fusion.8
  143.8 0.6 convolution_subtract_fusion.3
  144.4 0.6 convolution_add_fusion.3
  145.5 0.5 fusion.21
  146.6 0.5 fusion.2
  147.6 8.2 %copy.41 = f32[1,2,8,2,4096]{2,3,1,0,4:T(2,128)} copy(f32[1,2,8,2,4096]{4,2,3,1,0:T(8,128)S(1)} %pad_maximum_fusion.1) | data formatting | bytes 1048576 | tf_op jit(solution)/shard_map/stack | solution.py:90
  155.8 14.9 %reshape.304 = f32[32,1,4096]{2,1,0:T(1,128)S(1)} reshape(f32[4096,1,2,2,8]{4,3,2,1,0:T(2,128)} %bitcast.151) | data formatting | bytes 1048576
  170.7 41.4 %all_to_all.51 = f32[32,1,4096]{2,1,0:T(1,128)S(1)} all-to-all(f32[32,1,4096]{2,1,0:T(1,128)S(1)} %reshape.304), channel_id=1, replica_groups=mesh['context'=32,'tensor'=16] {'context'}, dimensions={0} | all-to-all | bytes 1048576 | tf_op jit(solution)/shard_map/all_to_all | solution.py:91
  212.2 0.5 broadcast.373
  212.7 1.9 reduce
  214.6 14.0 %reshape.305 = f32[4096,1,2,2,8]{4,3,2,1,0:T(2,128)} reshape(f32[32,4096]{1,0:T(8,128)S(1)} %reduce) | data formatting | bytes 1048576
  228.6 9.6 %copy.42 = f32[1,2,8,2,32,128]{5,3,4,2,1,0:T(2,128)S(1)} copy(f32[1,2,8,2,32,128]{2,3,1,5,4,0:T(2,128)} %bitcast.152) | data formatting | bytes 1048576 | tf_op jit(solution)/shard_map/all_to_all | solution.py:91
  240.0 21.5 %all_to_all.52 = f32[2,8,32,128]{3,1,0,2:T(8,128)S(1)} all-to-all(f32[2,8,32,128]{3,1,0,2:T(8,128)S(1)} %copy.43), channel_id=1, replica_groups=mesh['context'=32,'tensor'=16] {'context'}, dimensions={2} | all-to-all | bytes 524288 | tf_op jit(solution)/shard_map/all_to_all | solution.py:97
  261.5 0.7 slice_bitcast_fusion.8
  (21 shorter events, 4.4 us)
Async XLA Ops:
  57.5 74.7 %all-to-all-start.1 = ((f32[3,2,8,64,128]{4,2,0,1,3:T(8,128)}), f32[3,2,8,64,128]{4,2,0,1,3:T(8,128)S(1)}, u32[]{:S(2)}, u32[]{:S(2)}) async-start(f32[3,2,8,64,128]{4,2,0,1,3:T(8,128)} %copy.31), calls=%async_computation.1 | async-start | bytes 3145728 | tf_op jit(solution)/shard_map/all_to_all | solution.py:70
where the time goes:
time: 263 us; the launch traced here: 262 us
  blocking collectives  115 us (44%)
  waiting for transfers between devices  69.5 us (26%)
  local copies, waits for them, and re-layouts  51.8 us (20%)
  matrix products  16.4 us (6%)
  other arithmetic  4.67 us (2%)
  starting transfers between devices  4.15 us (2%)
    all_to_all x1, waiting for transfers between devices, per_device(): lax.all_to_all(columns, 'context', split_axis=3, concat_axis=4, tiled=True)  69.5 us
    all_to_all x1, blocking collectives, per_device(): lax.all_to_all(signals.reshape(3, channels, context_size, column_len), 'c...  51.7 us
    all_to_all x1, blocking collectives, per_device(): lax.all_to_all(rows_back, 'context', split_axis=4, concat_axis=3, tiled=T...  41.4 us
    unnamed x2, local copies, waits for them, and re-layouts  29 us
    all_to_all x1, blocking collectives, per_device(): lax.all_to_all(folded, 'context', split_axis=2, concat_axis=3, tiled=True)  21.5 us
    all_to_all x2, local copies, waits for them, and re-layouts, per_device(): lax.all_to_all(rows_back, 'context', split_axis=4, concat_axis=3, tiled=T...  10.2 us
    another operation x1, local copies, waits for them, and re-layouts, per_device(): rows_back = jnp.stack([untwisted[0], untwisted[1]], axis=1)  8.17 us
  transfers between devices with their start and end apart: 1, of which 1 were waited for; matrix products, arithmetic and copies ran while one was open for 0% of the time, Pallas kernels for 0%

commit v1 on v0

v1 whole, which is shorter than its diff:
```python
import functools

import jax
import jax.numpy as jnp
import numpy as np
from jax import lax
from jax.experimental import pallas as pl
from jax.experimental.pallas import tpu as pltpu
from jax.sharding import PartitionSpec as P

PLANE = 16
HALF = 4
GROUP = 8
A, B = 64, 128
BLOCK = A * B


def split_bf16(table):
    high = table.astype(jnp.bfloat16)
    low = (table - high.astype(np.float64)).astype(jnp.bfloat16)
    return high, low


def tables():
    a, b = np.arange(A), np.arange(B)
    first = 2 * np.pi * (np.arange(A)[:, None] + 0.25) * a[None, :] / A
    last = 2 * np.pi * (np.arange(B)[:, None] * b[None, :] % B) / B
    twist = -2 * np.pi * (np.arange(A)[:, None] + 0.25) * b[None, :] / BLOCK
    fwd1 = np.concatenate([np.cos(first), -np.sin(first)], 0)
    fwd2 = np.block([[np.cos(last), -np.sin(last)], [np.sin(last), np.cos(last)]])
    inv1 = np.block([[np.cos(last), np.sin(last)], [-np.sin(last), np.cos(last)]])
    inv2 = np.concatenate([np.cos(first).T, -np.sin(first).T], 1) / BLOCK
    h, l = split_bf16(fwd1)
    fwd1 = np.concatenate([h, l, h], 1)
    h, l = split_bf16(fwd2)
    fwd2 = np.concatenate([h, l, h], 0)
    h, l = split_bf16(inv1)
    inv1 = np.concatenate([h, l, h], 0)
    h, l = split_bf16(inv2)
    inv2 = np.concatenate([h, l, h], 1)
    turn = np.stack([np.cos(twist), np.sin(twist)]).astype(np.float32)
    return fwd1, fwd2, inv1, inv2, turn


def tripled(value, axis):
    high = value.astype(jnp.bfloat16)
    low = (value - high.astype(jnp.float32)).astype(jnp.bfloat16)
    return jnp.concatenate([high, high, low], axis=axis)


def mm(left, right):
    return jnp.dot(left, right, preferred_element_type=jnp.float32)


def kernel(
    x_hbm, g_hbm, r_hbm, fwd1_hbm, fwd2_hbm, inv1_hbm, inv2_hbm, turn_hbm,
    dx_ref, dr_ref,
    raw, rows, mine, vin, fsend, frecv, bsend, brecv, yout, yrecv, orow,
    fwd1, fwd2, inv1, inv2, turn,
    in_sem, z1s, z1r, fs, fr, bs, br, z2s, z2r,
):
    ctx = lax.axis_index("context")
    h = lax.rem(ctx, 2)
    m = lax.div(ctx, 2)
    gx, gy = lax.div(m, 4), lax.rem(m, 4)
    group = lax.rem(gx + gy, 2)
    place = 2 * gx + lax.div(gy, 2)
    partner = {"context": 2 * m + 1 - h}

    barrier = pltpu.get_barrier_semaphore()
    pl.semaphore_signal(barrier, 1, device_id=partner)
    for i in range(1, PLANE):
        pl.semaphore_signal(barrier, 1, device_id={"context": 2 * lax.rem(m + i, PLANE) + h})

    loads = [
        pltpu.make_async_copy(src, dst, in_sem.at[i])
        for i, (src, dst) in enumerate(
            [(x_hbm, raw.at[0]), (g_hbm, raw.at[1]), (r_hbm, raw.at[2]),
             (fwd1_hbm, fwd1), (fwd2_hbm, fwd2), (inv1_hbm, inv1), (inv2_hbm, inv2), (turn_hbm, turn)]
        )
    ]
    for copy in loads:
        copy.start()
    for copy in loads[:3]:
        copy.wait()
    for s in range(3):
        for a in range(32):
            rows[s, 8 * a : 8 * a + 8, :] = raw[s, :, 128 * a : 128 * a + 128]
    for s in range(3):
        for ch in range(8):
            mine[ch, s] = rows[s, pl.ds(ch, 32, stride=8), :]
    for copy in loads[3:]:
        copy.wait()

    def z1(c):
        return pltpu.make_async_remote_copy(
            mine.at[HALF * (1 - h) + c], vin.at[c, h], z1s.at[c], z1r.at[c], device_id=partner
        )

    def z1_in(c):
        return pltpu.make_async_remote_copy(
            mine.at[HALF * (1 - h) + c], vin.at[c, 1 - h], z1s.at[c], z1r.at[c], device_id=partner
        )

    def z2(c):
        return pltpu.make_async_remote_copy(
            yout.at[c, 1 - h], yrecv.at[c], z2s.at[c], z2r.at[c], device_id=partner
        )

    def member(q, side):
        x = lax.div(q, 2)
        return 4 * x + 2 * lax.rem(q, 2) + lax.rem(side + x, 2)

    def fwd(c, q):
        return pltpu.make_async_remote_copy(
            fsend.at[c, q], frecv.at[lax.div(c, 2), m], fs.at[c, q], fr.at[lax.div(c, 2), m],
            device_id={"context": 2 * member(q, lax.rem(c, 2)) + h},
        )

    def fwd_in(slot, src):
        return pltpu.make_async_remote_copy(
            fsend.at[0, 0], frecv.at[slot, src], fs.at[0, 0], fr.at[slot, src],
            device_id={"context": 2 * src + h},
        )

    def back(c, k):
        return pltpu.make_async_remote_copy(
            bsend.at[lax.div(c, 2), k], brecv.at[c, place], bs.at[lax.div(c, 2), k], br.at[c, place],
            device_id={"context": 2 * k + h},
        )

    def back_in(c, q):
        return pltpu.make_async_remote_copy(
            bsend.at[0, 0], brecv.at[c, q], bs.at[0, 0], br.at[c, q],
            device_id={"context": 2 * member(q, lax.rem(c, 2)) + h},
        )

    pl.semaphore_wait(barrier, PLANE)

    @pl.loop(0, HALF)
    def _(c):
        z1(c).start()

    @pl.loop(0, HALF)
    def _(c):
        vin[c, h] = mine[HALF * h + c]

    def forward(c):
        z1_in(c).wait_recv()
        value = jnp.concatenate(
            [jnp.concatenate([vin[c, half, s] for half in range(2)], axis=0) for s in range(3)], axis=1
        )
        part = mm(fwd1[...], tripled(value, 0))
        tr, ti = turn[0], turn[1]
        turned = []
        for s in range(3):
            re, im = part[:A, B * s : B * (s + 1)], part[A:, B * s : B * (s + 1)]
            turned.append(jnp.concatenate([re * tr - im * ti, re * ti + im * tr], axis=1))
        spec = mm(tripled(jnp.concatenate(turned, axis=0), 1), fwd2[...])
        for q in range(GROUP):
            for s in range(3):
                fsend[c, q, s] = spec[A * s + 8 * q : A * s + 8 * q + 8, :]

        @pl.loop(0, GROUP)
        def _(q):
            @pl.when(member(q, lax.rem(c, 2)) != m)
            def _():
                fwd(c, q).start()

    def middle(c):
        slot = lax.div(c, 2)
        frecv[slot, m] = fsend[c, place]

        @pl.loop(0, PLANE)
        def _(src):
            @pl.when(src != m)
            def _():
                fwd_in(slot, src).wait_recv()

        def spec(n, s):
            return frecv[slot, n, s, :, :B], frecv[slot, n, s, :, B:]

        folded = []
        for n in range(PLANE):
            re, im = spec(n, 1)
            if n + 1 < PLANE:
                next_re, next_im = spec(n + 1, 1)
                re, im = re + next_im, im - next_re
            folded.append((re, im))
        for k in range(PLANE):
            for out, s in enumerate((2, 0)):
                total_re = total_im = None
                for n in range(PLANE - k):
                    re, im = spec(n, s)
                    wr, wi = folded[n + k]
                    add_re, add_im = re * wr + im * wi, re * wi - im * wr
                    total_re = add_re if total_re is None else total_re + add_re
                    total_im = add_im if total_im is None else total_im + add_im
                bsend[slot, k, out, :, :B] = total_re
                bsend[slot, k, out, :, B:] = total_im

        @pl.loop(0, PLANE)
        def _(k):
            @pl.when(k != m)
            def _():
                back(c, k).start()

        brecv[c, place] = bsend[slot, m]

    def inverse(c):
        @pl.loop(0, GROUP)
        def _(q):
            @pl.when(member(q, lax.rem(c, 2)) != m)
            def _():
                back_in(c, q).wait_recv()

        value = jnp.concatenate([brecv[c, q, out] for out in range(2) for q in range(GROUP)], axis=0)
        part = mm(tripled(value, 1), inv1[...])
        tr, ti = turn[0], turn[1]
        turned = []
        for out in range(2):
            re, im = part[A * out : A * (out + 1), :B], part[A * out : A * (out + 1), B:]
            turned.append(jnp.concatenate([re * tr + im * ti, im * tr - re * ti], axis=0))
        y = mm(inv2[...], tripled(jnp.concatenate(turned, axis=1), 0))
        for out in range(2):
            for half in range(2):
                yout[c, half, out] = y[32 * half : 32 * (half + 1), B * out : B * (out + 1)]
        z2(c).start()

    @pl.loop(0, HALF)
    def _(c):
        forward(c)

        @pl.when(lax.rem(c, 2) == group)
        def _():
            middle(c)

        @pl.when(c > 0)
        def _():
            inverse(c - 1)

    inverse(HALF - 1)

    @pl.loop(0, HALF)
    def _(c):
        for out in range(2):
            orow[out, pl.ds(HALF * h + c, 32, stride=8), :] = yout[c, h, out]

    @pl.loop(0, HALF)
    def _(c):
        z2(c).wait_recv()
        for out in range(2):
            orow[out, pl.ds(HALF * (1 - h) + c, 32, stride=8), :] = yrecv[c, out]

    for a in range(32):
        dx_ref[:, 128 * a : 128 * a + 128] = orow[0, 8 * a : 8 * a + 8, :]
        dr_ref[:, 128 * a : 128 * a + 128] = orow[1, 8 * a : 8 * a + 8, :]

    @pl.loop(0, HALF)
    def _(c):
        z1(c).wait_send()
        z2(c).wait_send()

        @pl.loop(0, GROUP)
        def _(q):
            @pl.when(member(q, lax.rem(c, 2)) != m)
            def _():
                fwd(c, q).wait_send()

        @pl.when(lax.rem(c, 2) == group)
        def _():
            @pl.loop(0, PLANE)
            def _(k):
                @pl.when(k != m)
                def _():
                    back(c, k).wait_send()


def per_device(inputs, grads, response):
    consts = tables()
    f32, bf16 = jnp.float32, jnp.bfloat16
    vmem, dma = pltpu.VMEM, pltpu.SemaphoreType.DMA
    return pl.pallas_call(
        kernel,
        out_shape=(jax.ShapeDtypeStruct(inputs.shape, f32),) * 2,
        in_specs=[pl.BlockSpec(memory_space=pl.ANY)] * 8,
        out_specs=(pl.BlockSpec(memory_space=vmem),) * 2,
        scratch_shapes=[
            vmem((3, 8, 4096), f32),
            vmem((3, 256, 128), f32),
            vmem((8, 3, 32, 128), f32),
            vmem((HALF, 2, 3, 32, 128), f32),
            vmem((HALF, GROUP, 3, 8, 2 * B), f32),
            vmem((2, PLANE, 3, 8, 2 * B), f32),
            vmem((2, PLANE, 2, 8, 2 * B), f32),
            vmem((HALF, GROUP, 2, 8, 2 * B), f32),
            vmem((HALF, 2, 2, 32, 128), f32),
            vmem((HALF, 2, 32, 128), f32),
            vmem((2, 256, 128), f32),
            vmem((2 * A, 3 * A), bf16),
            vmem((6 * B, 2 * B), bf16),
            vmem((6 * B, 2 * B), bf16),
            vmem((A, 6 * A), bf16),
            vmem((2, A, B), f32),
            dma((8,)),
            dma((HALF,)), dma((HALF,)),
            dma((HALF, GROUP)), dma((2, PLANE)),
            dma((2, PLANE)), dma((HALF, GROUP)),
            dma((HALF,)), dma((HALF,)),
        ],
        compiler_params=pltpu.CompilerParams(collective_id=0, has_side_effects=True),
        name="hyena_backward",
    )(inputs, grads, response, *(jnp.asarray(t) for t in consts))


def solution(mesh):
    return jax.shard_map(
        per_device,
        mesh=mesh,
        in_specs=(P("tensor", "context"),) * 3,
        out_specs=(P("tensor", "context"),) * 2,
        check_vma=False,
    )
```

time: 263 us -> 80.9 us (0.31)
  the two profiles are of different devices: /device:TPU:32 before, /device:TPU:36 now
where the time goes in v1:
time: 80.9 us; the launch traced here: 80.7 us
  Pallas kernels  77.8 us (96%)
  local copies, waits for them, and re-layouts  2.26 us (3%)
    pallas_call x1, Pallas kernels, per_device(): pl.pallas_call(kernel, out_shape=(jax.ShapeDtypeStruct(inputs.shape, f32)...  77.8 us
    unnamed x4, local copies, waits for them, and re-layouts  2.26 us

profile of v1, /device:TPU:36, one launch (start us, length us, event | category | flops | bytes accessed | tf_op | source)
XLA Modules:
  0.0 80.7 jit_solution(14379150349533372563)
XLA Ops:
  0.6 77.8 %hyena_backward.1 = (f32[8,4096]{1,0:T(8,128)}, f32[8,4096]{1,0:T(8,128)}) custom-call(f32[8,4096]{1,0:T(8,128)} %x_hbm.1, f32[8,4096]{1,0:T(8,128)} %g_hbm.1, f32[8,4096]{1,0:T(8,128)} %r_hbm.1, bf16[128,192]{1,0:T(8,128)(2,1)} %constant.10.clone.fwd1_hbm, bf16[768,256]{1,0:T(8,128)(2,1)} %constant.11.clone.fwd2_hbm, ...), custom_call_target="tpu_custom_call" | custom-call | tf_op jit(solution)/shard_map/hyena_backward/pallas_call | solution.py:283
  78.4 0.0 copy-start
  78.4 1.6 %copy.12 = f32[8,4096]{1,0:T(8,128)} copy(f32[8,4096]{1,0:T(8,128)} %get-tuple-element.4) | data formatting | bytes 262144
  80.0 0.0 copy-done
  80.1 0.7 copy.13
Async XLA Ops:
  78.4 1.6 %copy-start = (f32[8,4096]{1,0:T(8,128)S(1)}, f32[8,4096]{1,0:T(8,128)}, u32[]{:S(2)}) copy-start(f32[8,4096]{1,0:T(8,128)} %get-tuple-element.5) | copy-start | bytes 393220

commit v2 on v1

--- a/solution.py
+++ b/solution.py
@@ -13,6 +13,8 @@
 GROUP = 8
 A, B = 64, 128
 BLOCK = A * B
+Z1_CUT = 3
+Z2_CUT = 2
 
 
 def split_bf16(table):
@@ -88,23 +90,27 @@
             rows[s, 8 * a : 8 * a + 8, :] = raw[s, :, 128 * a : 128 * a + 128]
     for s in range(3):
         for ch in range(8):
-            mine[ch, s] = rows[s, pl.ds(ch, 32, stride=8), :]
+            value = rows[s, pl.ds(ch, 32, stride=8), :]
+            size = 96 // Z1_CUT
+            for at in range(0, 32, min(32, size)):
+                row = 32 * s + at
+                mine[ch, row // size, row % size : row % size + min(32, size)] = value[at : at + min(32, size)]
     for copy in loads[3:]:
         copy.wait()
 
-    def z1(c):
-        return pltpu.make_async_remote_copy(
-            mine.at[HALF * (1 - h) + c], vin.at[c, h], z1s.at[c], z1r.at[c], device_id=partner
-        )
-
-    def z1_in(c):
-        return pltpu.make_async_remote_copy(
-            mine.at[HALF * (1 - h) + c], vin.at[c, 1 - h], z1s.at[c], z1r.at[c], device_id=partner
-        )
-
-    def z2(c):
-        return pltpu.make_async_remote_copy(
-            yout.at[c, 1 - h], yrecv.at[c], z2s.at[c], z2r.at[c], device_id=partner
+    def z1(c, i):
+        return pltpu.make_async_remote_copy(
+            mine.at[HALF * (1 - h) + c, i], vin.at[c, h, i], z1s.at[c, i], z1r.at[c, i], device_id=partner
+        )
+
+    def z1_in(c, i):
+        return pltpu.make_async_remote_copy(
+            mine.at[HALF * (1 - h) + c, i], vin.at[c, 1 - h, i], z1s.at[c, i], z1r.at[c, i], device_id=partner
+        )
+
+    def z2(c, i):
+        return pltpu.make_async_remote_copy(
+            yout.at[c, 1 - h, i], yrecv.at[c, i], z2s.at[c, i], z2r.at[c, i], device_id=partner
         )
 
     def member(q, side):
@@ -139,16 +145,22 @@
 
     @pl.loop(0, HALF)
     def _(c):
-        z1(c).start()
+        for i in range(Z1_CUT):
+            z1(c, i).start()
 
     @pl.loop(0, HALF)
     def _(c):
         vin[c, h] = mine[HALF * h + c]
 
     def forward(c):
-        z1_in(c).wait_recv()
+        for i in range(Z1_CUT):
+            z1_in(c, i).wait_recv()
         value = jnp.concatenate(
-            [jnp.concatenate([vin[c, half, s] for half in range(2)], axis=0) for s in range(3)], axis=1
+            [
+                jnp.concatenate([vin[c, half].reshape(96, B)[32 * s : 32 * s + 32] for half in range(2)], axis=0)
+                for s in range(3)
+            ],
+            axis=1,
         )
         part = mm(fwd1[...], tripled(value, 0))
         tr, ti = turn[0], turn[1]
@@ -224,33 +236,39 @@
         y = mm(inv2[...], tripled(jnp.concatenate(turned, axis=1), 0))
         for out in range(2):
             for half in range(2):
-                yout[c, half, out] = y[32 * half : 32 * (half + 1), B * out : B * (out + 1)]
-        z2(c).start()
-
-    @pl.loop(0, HALF)
-    def _(c):
-        forward(c)
-
-        @pl.when(lax.rem(c, 2) == group)
+                size = 64 // Z2_CUT
+                value = y[32 * half : 32 * (half + 1), B * out : B * (out + 1)]
+                for at in range(0, 32, min(32, size)):
+                    row = 32 * out + at
+                    yout[c, half, row // size, row % size : row % size + min(32, size)] = value[at : at + min(32, size)]
+        for i in range(Z2_CUT):
+            z2(c, i).start()
+
+    @pl.loop(0, HALF + 2)
+    def _(step):
+        @pl.when(step < HALF)
         def _():
-            middle(c)
-
-        @pl.when(c > 0)
+            forward(step)
+
+        @pl.when((step >= 1) & (step <= HALF) & (lax.rem(step + 1, 2) == group))
         def _():
-            inverse(c - 1)
-
-    inverse(HALF - 1)
+            middle(step - 1)
+
+        @pl.when(step >= 2)
+        def _():
+            inverse(step - 2)
 
     @pl.loop(0, HALF)
     def _(c):
         for out in range(2):
-            orow[out, pl.ds(HALF * h + c, 32, stride=8), :] = yout[c, h, out]
-
-    @pl.loop(0, HALF)
-    def _(c):
-        z2(c).wait_recv()
+            orow[out, pl.ds(HALF * h + c, 32, stride=8), :] = yout[c, h].reshape(64, B)[32 * out : 32 * out + 32]
+
+    @pl.loop(0, HALF)
+    def _(c):
+        for i in range(Z2_CUT):
+            z2(c, i).wait_recv()
         for out in range(2):
-            orow[out, pl.ds(HALF * (1 - h) + c, 32, stride=8), :] = yrecv[c, out]
+            orow[out, pl.ds(HALF * (1 - h) + c, 32, stride=8), :] = yrecv[c].reshape(64, B)[32 * out : 32 * out + 32]
 
     for a in range(32):
         dx_ref[:, 128 * a : 128 * a + 128] = orow[0, 8 * a : 8 * a + 8, :]
@@ -258,8 +276,10 @@
 
     @pl.loop(0, HALF)
     def _(c):
-        z1(c).wait_send()
-        z2(c).wait_send()
+        for i in range(Z1_CUT):
+            z1(c, i).wait_send()
+        for i in range(Z2_CUT):
+            z2(c, i).wait_send()
 
         @pl.loop(0, GROUP)
         def _(q):
@@ -288,14 +308,14 @@
         scratch_shapes=[
             vmem((3, 8, 4096), f32),
             vmem((3, 256, 128), f32),
-            vmem((8, 3, 32, 128), f32),
-            vmem((HALF, 2, 3, 32, 128), f32),
+            vmem((8, Z1_CUT, 96 // Z1_CUT, 128), f32),
+            vmem((HALF, 2, Z1_CUT, 96 // Z1_CUT, 128), f32),
             vmem((HALF, GROUP, 3, 8, 2 * B), f32),
             vmem((2, PLANE, 3, 8, 2 * B), f32),
             vmem((2, PLANE, 2, 8, 2 * B), f32),
             vmem((HALF, GROUP, 2, 8, 2 * B), f32),
-            vmem((HALF, 2, 2, 32, 128), f32),
-            vmem((HALF, 2, 32, 128), f32),
+            vmem((HALF, 2, Z2_CUT, 64 // Z2_CUT, 128), f32),
+            vmem((HALF, Z2_CUT, 64 // Z2_CUT, 128), f32),
             vmem((2, 256, 128), f32),
             vmem((2 * A, 3 * A), bf16),
             vmem((6 * B, 2 * B), bf16),
@@ -303,10 +323,10 @@
             vmem((A, 6 * A), bf16),
             vmem((2, A, B), f32),
             dma((8,)),
-            dma((HALF,)), dma((HALF,)),
+            dma((HALF, Z1_CUT)), dma((HALF, Z1_CUT)),
             dma((HALF, GROUP)), dma((2, PLANE)),
             dma((2, PLANE)), dma((HALF, GROUP)),
-            dma((HALF,)), dma((HALF,)),
+            dma((HALF, Z2_CUT)), dma((HALF, Z2_CUT)),
         ],
         compiler_params=pltpu.CompilerParams(collective_id=0, has_side_effects=True),
         name="hyena_backward",

time: 80.9 us -> 70.9 us (0.88)
  the two profiles are of different devices: /device:TPU:36 before, /device:TPU:32 now
where the time goes in v2:
time: 70.9 us; the launch traced here: 70.8 us
  Pallas kernels  67.9 us (96%)
  local copies, waits for them, and re-layouts  2.26 us (3%)
    pallas_call x1, Pallas kernels, per_device(): pl.pallas_call(kernel, out_shape=(jax.ShapeDtypeStruct(inputs.shape, f32)...  67.9 us
    unnamed x4, local copies, waits for them, and re-layouts  2.26 us

profile of v2, /device:TPU:32, one launch (start us, length us, event | category | flops | bytes accessed | tf_op | source)
XLA Modules:
  0.0 70.8 jit_solution(1891188426565456308)
XLA Ops:
  0.6 67.9 %hyena_backward.1 = (f32[8,4096]{1,0:T(8,128)}, f32[8,4096]{1,0:T(8,128)}) custom-call(f32[8,4096]{1,0:T(8,128)} %x_hbm.1, f32[8,4096]{1,0:T(8,128)} %g_hbm.1, f32[8,4096]{1,0:T(8,128)} %r_hbm.1, bf16[128,192]{1,0:T(8,128)(2,1)} %constant.10.clone.fwd1_hbm, bf16[768,256]{1,0:T(8,128)(2,1)} %constant.11.clone.fwd2_hbm, ...), custom_call_target="tpu_custom_call" | custom-call | tf_op jit(solution)/shard_map/hyena_backward/pallas_call | solution.py:303
  68.5 0.0 copy-start
  68.5 1.6 %copy.12 = f32[8,4096]{1,0:T(8,128)} copy(f32[8,4096]{1,0:T(8,128)} %get-tuple-element.4) | data formatting | bytes 262144
  70.1 0.0 copy-done
  70.1 0.7 copy.13
Async XLA Ops:
  68.5 1.6 %copy-start = (f32[8,4096]{1,0:T(8,128)S(1)}, f32[8,4096]{1,0:T(8,128)}, u32[]{:S(2)}) copy-start(f32[8,4096]{1,0:T(8,128)} %get-tuple-element.5) | copy-start | bytes 393220

commit v3 on v2

v3 whole, which is shorter than its diff:
```python
import functools

import jax
import jax.numpy as jnp
import numpy as np
from jax import lax
from jax.experimental import pallas as pl
from jax.experimental.pallas import tpu as pltpu
from jax.sharding import PartitionSpec as P

PLANE = 16
HALF = 4
GROUP = 8
A, B = 64, 128
BLOCK = A * B
Z1_CUT = 3
M_LAG, I_LAG = 2, 4


def split_bf16(table):
    high = table.astype(jnp.bfloat16)
    low = (table - high.astype(np.float64)).astype(jnp.bfloat16)
    return high, low


def tables():
    a, b = np.arange(A), np.arange(B)
    first = 2 * np.pi * (np.arange(A)[:, None] + 0.25) * a[None, :] / A
    last = 2 * np.pi * (np.arange(B)[:, None] * b[None, :] % B) / B
    twist = -2 * np.pi * (np.arange(A)[:, None] + 0.25) * b[None, :] / BLOCK
    fwd1 = np.concatenate([np.cos(first), -np.sin(first)], 0)
    fwd2 = np.block([[np.cos(last), -np.sin(last)], [np.sin(last), np.cos(last)]])
    inv1 = np.block([[np.cos(last), np.sin(last)], [-np.sin(last), np.cos(last)]])
    inv2 = np.concatenate([np.cos(first).T, -np.sin(first).T], 1) / BLOCK
    h, l = split_bf16(fwd1)
    fwd1 = np.concatenate([h, l, h], 1)
    h, l = split_bf16(fwd2)
    fwd2 = np.concatenate([h, l, h], 0)
    h, l = split_bf16(inv1)
    inv1 = np.concatenate([h, l, h], 0)
    h, l = split_bf16(inv2)
    inv2 = np.concatenate([h, l, h], 1)
    turn = np.stack([np.cos(twist), np.sin(twist)]).astype(np.float32)
    return fwd1, fwd2, inv1, inv2, turn


def tripled(value, axis):
    high = value.astype(jnp.bfloat16)
    low = (value - high.astype(jnp.float32)).astype(jnp.bfloat16)
    return jnp.concatenate([high, high, low], axis=axis)


def mm(left, right):
    return jnp.dot(left, right, preferred_element_type=jnp.float32)


def kernel(
    x_hbm, g_hbm, r_hbm, fwd1_hbm, fwd2_hbm, inv1_hbm, inv2_hbm, turn_hbm,
    dx_ref, dr_ref,
    raw, rows, mine, vin, fsend, frecv, bsend, brecv, yout, yrecv, orow,
    fwd1, fwd2, inv1, inv2, turn, passing,
    in_sem, z1s, z1r, ps, pr, fs, fr, bs, br, z2s, z2r,
):
    ctx = lax.axis_index("context")
    tens = lax.axis_index("tensor")
    h = ctx & 1
    m = ctx >> 1
    gx, gy = m >> 2, m & 3
    group = (gx + gy) & 1
    place = 2 * gx + (gy >> 1)
    z = 8 * h + (tens >> 1)
    partner = {"context": ctx ^ 1}

    def along_z(far):
        to = (z + far) & 15
        return {"context": 2 * m + (to >> 3), "tensor": 2 * (to & 7) + (tens & 1)}

    barrier = pltpu.get_barrier_semaphore()
    pl.semaphore_signal(barrier, 1, device_id=along_z(4))
    pl.semaphore_signal(barrier, 1, device_id=along_z(12))
    for i in range(1, PLANE):
        pl.semaphore_signal(barrier, 1, device_id={"context": 2 * ((m + i) & 15) + h})

    loads = [
        pltpu.make_async_copy(src, dst, in_sem.at[i])
        for i, (src, dst) in enumerate(
            [(x_hbm, raw.at[0]), (g_hbm, raw.at[1]), (r_hbm, raw.at[2]),
             (fwd1_hbm, fwd1), (fwd2_hbm, fwd2), (inv1_hbm, inv1), (inv2_hbm, inv2), (turn_hbm, turn)]
        )
    ]
    for copy in loads:
        copy.start()
    for copy in loads[:3]:
        copy.wait()
    for s in range(3):
        for a in range(32):
            rows[s, 8 * a : 8 * a + 8, :] = raw[s, :, 128 * a : 128 * a + 128]
    for s in range(3):
        for ch in range(8):
            mine[ch, s] = rows[s, pl.ds(ch, 32, stride=8), :]

    def way(c, i):
        return 4 + 8 * ((c + i) & 1)

    def z1(c, i):
        return pltpu.make_async_remote_copy(
            mine.at[HALF * (1 - h) + c, i], passing.at[c, i], z1s.at[c, i], pr.at[c, i], device_id=along_z(way(c, i))
        )

    def z1_on(c, i):
        side = ((z + way(c, i)) & 15) >> 3
        return pltpu.make_async_remote_copy(
            passing.at[c, i], vin.at[c, 1 - side, i], ps.at[c, i], z1r.at[c, i], device_id=along_z(way(c, i))
        )

    def z1_in(c, i):
        return pltpu.make_async_remote_copy(
            passing.at[c, i], vin.at[c, 1 - h, i], ps.at[c, i], z1r.at[c, i], device_id=along_z(way(c, i))
        )

    def z2(c, i):
        return pltpu.make_async_remote_copy(
            yout.at[c, 1 - h, i], yrecv.at[c, i], z2s.at[c, i], z2r.at[c, i], device_id=partner
        )

    def member(q, side):
        x = q >> 1
        return 4 * x + 2 * (q & 1) + ((side + x) & 1)

    def fwd(c, q):
        return pltpu.make_async_remote_copy(
            fsend.at[c, q], frecv.at[c >> 1, m], fs.at[c], fr.at[c >> 1],
            device_id={"context": 2 * member(q, c & 1) + h},
        )

    def fwd_all(c, count):
        return pltpu.make_async_remote_copy(
            fsend.at[c, pl.ds(0, count)], frecv.at[c >> 1, pl.ds(0, count)], fs.at[c], fr.at[c >> 1], device_id=partner
        )

    def fwd_in(slot):
        part = frecv.at[slot, pl.ds(0, PLANE - 1)]
        return pltpu.make_async_remote_copy(part, part, fs.at[0], fr.at[slot], device_id=partner)

    def back(c, k):
        return pltpu.make_async_remote_copy(
            bsend.at[c >> 1, k], brecv.at[c, place], bs.at[c >> 1], br.at[c], device_id={"context": 2 * k + h}
        )

    def back_in(c, count):
        part = brecv.at[c, pl.ds(0, count)]
        return pltpu.make_async_remote_copy(part, part, bs.at[0], br.at[c], device_id=partner)

    def back_out(slot):
        part = bsend.at[slot, pl.ds(0, PLANE - 1)]
        return pltpu.make_async_remote_copy(part, part, bs.at[slot], br.at[0], device_id=partner)

    pl.semaphore_wait(barrier, PLANE + 1)

    @pl.loop(0, HALF)
    def _(c):
        for i in range(Z1_CUT):
            z1(c, i).start()

    @pl.loop(0, HALF)
    def _(c):
        vin[c, h] = mine[HALF * h + c]

    for copy in loads[3:]:
        copy.wait()

    @pl.loop(0, HALF)
    def _(c):
        for i in range(Z1_CUT):
            z1(c, i).wait_recv()
            z1_on(c, i).start()

    def forward(c):
        for i in range(Z1_CUT):
            z1_in(c, i).wait_recv()
        value = jnp.concatenate(
            [jnp.concatenate([vin[c, half, s] for half in range(2)], axis=0) for s in range(3)], axis=1
        )
        part = mm(fwd1[...], tripled(value, 0))
        tr, ti = turn[0], turn[1]
        turned = []
        for s in range(3):
            re, im = part[:A, B * s : B * (s + 1)], part[A:, B * s : B * (s + 1)]
            turned.append(jnp.concatenate([re * tr - im * ti, re * ti + im * tr], axis=1))
        spec = mm(tripled(jnp.concatenate(turned, axis=0), 1), fwd2[...])
        for q in range(GROUP):
            for s in range(3):
                fsend[c, q, s] = spec[A * s + 8 * q : A * s + 8 * q + 8, :]

        for i in range(1, GROUP):
            fwd(c, (place + i) & 7).start()

        @pl.when((c & 1) != group)
        def _():
            fwd(c, place).start()

    def middle(c):
        slot = c >> 1
        frecv[slot, m] = fsend[c, place]
        fwd_in(slot).wait_recv()

        def spec(n, s):
            return frecv[slot, n, s, :, :B], frecv[slot, n, s, :, B:]

        folded = []
        for n in range(PLANE):
            re, im = spec(n, 1)
            if n + 1 < PLANE:
                next_re, next_im = spec(n + 1, 1)
                re, im = re + next_im, im - next_re
            folded.append((re, im))
        for k in range(PLANE):
            for out, s in enumerate((2, 0)):
                total_re = total_im = None
                for n in range(PLANE - k):
                    re, im = spec(n, s)
                    wr, wi = folded[n + k]
                    add_re, add_im = re * wr + im * wi, re * wi - im * wr
                    total_re = add_re if total_re is None else total_re + add_re
                    total_im = add_im if total_im is None else total_im + add_im
                bsend[slot, k, out, :, :B] = total_re
                bsend[slot, k, out, :, B:] = total_im
        for i in range(1, PLANE):
            back(c, (m + i) & 15).start()
        brecv[c, place] = bsend[slot, m]

    def inverse(c):
        @pl.when((c & 1) == group)
        def _():
            back_in(c, GROUP - 1).wait_recv()

        @pl.when((c & 1) != group)
        def _():
            back_in(c, GROUP).wait_recv()

        value = jnp.concatenate([brecv[c, q, out] for out in range(2) for q in range(GROUP)], axis=0)
        part = mm(tripled(value, 1), inv1[...])
        tr, ti = turn[0], turn[1]
        turned = []
        for out in range(2):
            re, im = part[A * out : A * (out + 1), :B], part[A * out : A * (out + 1), B:]
            turned.append(jnp.concatenate([re * tr + im * ti, im * tr - re * ti], axis=0))
        y = mm(inv2[...], tripled(jnp.concatenate(turned, axis=1), 0))
        for out in range(2):
            for half in range(2):
                yout[c, half, out] = y[32 * half : 32 * (half + 1), B * out : B * (out + 1)]
        for i in range(2):
            z2(c, i).start()

    @pl.loop(0, HALF + I_LAG)
    def _(step):
        @pl.when(step < HALF)
        def _():
            forward(step)

        @pl.when((step >= M_LAG) & (step < HALF + M_LAG) & (((step + M_LAG) & 1) == group))
        def _():
            middle(step - M_LAG)

        @pl.when(step >= I_LAG)
        def _():
            inverse(step - I_LAG)

    @pl.loop(0, HALF)
    def _(c):
        for i in range(Z1_CUT):
            z1(c, i).wait_send()
            z1_on(c, i).wait_send()

        @pl.when((c & 1) == group)
        def _():
            fwd_all(c, GROUP - 1).wait_send()
            back_out(c >> 1).wait_send()

        @pl.when((c & 1) != group)
        def _():
            fwd_all(c, GROUP).wait_send()

        for out in range(2):
            orow[out, pl.ds(HALF * h + c, 32, stride=8), :] = yout[c, h, out]

    @pl.loop(0, HALF)
    def _(c):
        for i in range(2):
            z2(c, i).wait_recv()
            orow[i, pl.ds(HALF * (1 - h) + c, 32, stride=8), :] = yrecv[c, i]

    for a in range(32):
        dx_ref[:, 128 * a : 128 * a + 128] = orow[0, 8 * a : 8 * a + 8, :]
        dr_ref[:, 128 * a : 128 * a + 128] = orow[1, 8 * a : 8 * a + 8, :]

    @pl.loop(0, HALF)
    def _(c):
        for i in range(2):
            z2(c, i).wait_send()


def per_device(inputs, grads, response):
    consts = tables()
    f32, bf16 = jnp.float32, jnp.bfloat16
    vmem, dma = pltpu.VMEM, pltpu.SemaphoreType.DMA
    return pl.pallas_call(
        kernel,
        out_shape=(jax.ShapeDtypeStruct(inputs.shape, f32),) * 2,
        in_specs=[pl.BlockSpec(memory_space=pl.ANY)] * 8,
        out_specs=(pl.BlockSpec(memory_space=vmem),) * 2,
        scratch_shapes=[
            vmem((3, 8, 4096), f32),
            vmem((3, 256, 128), f32),
            vmem((8, Z1_CUT, 32, 128), f32),
            vmem((HALF, 2, Z1_CUT, 32, 128), f32),
            vmem((HALF, GROUP, 3, 8, 2 * B), f32),
            vmem((2, PLANE, 3, 8, 2 * B), f32),
            vmem((2, PLANE, 2, 8, 2 * B), f32),
            vmem((HALF, GROUP, 2, 8, 2 * B), f32),
            vmem((HALF, 2, 2, 32, 128), f32),
            vmem((HALF, 2, 32, 128), f32),
            vmem((2, 256, 128), f32),
            vmem((2 * A, 3 * A), bf16),
            vmem((6 * B, 2 * B), bf16),
            vmem((6 * B, 2 * B), bf16),
            vmem((A, 6 * A), bf16),
            vmem((2, A, B), f32),
            vmem((HALF, Z1_CUT, 32, B), f32),
            dma((8,)),
            dma((HALF, Z1_CUT)), dma((HALF, Z1_CUT)),
            dma((HALF, Z1_CUT)), dma((HALF, Z1_CUT)),
            dma((HALF,)), dma((2,)),
            dma((2,)), dma((HALF,)),
            dma((HALF, 2)), dma((HALF, 2)),
        ],
        compiler_params=pltpu.CompilerParams(collective_id=0, has_side_effects=True),
        name="hyena_backward",
    )(inputs, grads, response, *(jnp.asarray(t) for t in consts))


def solution(mesh):
    return jax.shard_map(
        per_device,
        mesh=mesh,
        in_specs=(P("tensor", "context"),) * 3,
        out_specs=(P("tensor", "context"),) * 2,
        check_vma=False,
    )
```

time: 70.9 us -> 66.1 us (0.932)
  the two profiles are of different devices: /device:TPU:32 before, /device:TPU:8 now
where the time goes in v3:
time: 66.1 us; the launch traced here: 66 us
  Pallas kernels  63 us (95%)
  local copies, waits for them, and re-layouts  2.26 us (3%)
    pallas_call x1, Pallas kernels, per_device(): pl.pallas_call(kernel, out_shape=(jax.ShapeDtypeStruct(inputs.shape, f32)...  63 us
    unnamed x4, local copies, waits for them, and re-layouts  2.26 us

profile of v3, /device:TPU:8, one launch (start us, length us, event | category | flops | bytes accessed | tf_op | source)
XLA Modules:
  0.0 66.0 jit_solution(4070496665878930763)
XLA Ops:
  0.6 63.0 %hyena_backward.1 = (f32[8,4096]{1,0:T(8,128)}, f32[8,4096]{1,0:T(8,128)}) custom-call(f32[8,4096]{1,0:T(8,128)} %x_hbm.1, f32[8,4096]{1,0:T(8,128)} %g_hbm.1, f32[8,4096]{1,0:T(8,128)} %r_hbm.1, bf16[128,192]{1,0:T(8,128)(2,1)} %constant.10.clone.fwd1_hbm, bf16[768,256]{1,0:T(8,128)(2,1)} %constant.11.clone.fwd2_hbm, ...), custom_call_target="tpu_custom_call" | custom-call | tf_op jit(solution)/shard_map/hyena_backward/pallas_call | solution.py:307
  63.7 0.0 copy-start
  63.7 1.6 %copy.12 = f32[8,4096]{1,0:T(8,128)} copy(f32[8,4096]{1,0:T(8,128)} %get-tuple-element.4) | data formatting | bytes 262144
  65.3 0.0 copy-done
  65.3 0.7 copy.13
Async XLA Ops:
  63.7 1.6 %copy-start = (f32[8,4096]{1,0:T(8,128)S(1)}, f32[8,4096]{1,0:T(8,128)}, u32[]{:S(2)}) copy-start(f32[8,4096]{1,0:T(8,128)} %get-tuple-element.5) | copy-start | bytes 393220

commit v4 on v3

--- a/solution.py
+++ b/solution.py
@@ -14,7 +14,7 @@
 A, B = 64, 128
 BLOCK = A * B
 Z1_CUT = 3
-M_LAG, I_LAG = 2, 4
+I_LAG = 2
 
 
 def split_bf16(table):
@@ -56,10 +56,10 @@
 
 def kernel(
     x_hbm, g_hbm, r_hbm, fwd1_hbm, fwd2_hbm, inv1_hbm, inv2_hbm, turn_hbm,
-    dx_ref, dr_ref,
-    raw, rows, mine, vin, fsend, frecv, bsend, brecv, yout, yrecv, orow,
+    yout, yrecv,
+    raw, rows, mine, vin, fsend, frecv, bsend, brecv, ybuf,
     fwd1, fwd2, inv1, inv2, turn, passing,
-    in_sem, z1s, z1r, ps, pr, fs, fr, bs, br, z2s, z2r,
+    in_sem, z1s, z1r, ps, pr, fs, fr, bs, br, z2s, z2r, ready,
 ):
     ctx = lax.axis_index("context")
     tens = lax.axis_index("tensor")
@@ -71,15 +71,12 @@
     z = 8 * h + (tens >> 1)
     partner = {"context": ctx ^ 1}
 
+    def row_peer(i):
+        return {"context": 2 * ((m & 12) + ((m + i) & 3)) + h}
+
     def along_z(far):
         to = (z + far) & 15
         return {"context": 2 * m + (to >> 3), "tensor": 2 * (to & 7) + (tens & 1)}
-
-    barrier = pltpu.get_barrier_semaphore()
-    pl.semaphore_signal(barrier, 1, device_id=along_z(4))
-    pl.semaphore_signal(barrier, 1, device_id=along_z(12))
-    for i in range(1, PLANE):
-        pl.semaphore_signal(barrier, 1, device_id={"context": 2 * ((m + i) & 15) + h})
 
     loads = [
         pltpu.make_async_copy(src, dst, in_sem.at[i])
@@ -88,23 +85,27 @@
              (fwd1_hbm, fwd1), (fwd2_hbm, fwd2), (inv1_hbm, inv1), (inv2_hbm, inv2), (turn_hbm, turn)]
         )
     ]
-    for copy in loads:
+    for copy in loads[:3]:
         copy.start()
-    for copy in loads[:3]:
-        copy.wait()
+    barrier = pltpu.get_barrier_semaphore()
+    pl.semaphore_signal(barrier, 1, device_id=along_z(4))
+    pl.semaphore_signal(barrier, 1, device_id=along_z(12))
+    for i in range(1, 4):
+        pl.semaphore_signal(barrier, 1, device_id={"context": 2 * ((m + 4 * i) & 15) + h})
+        pl.semaphore_signal(barrier, 1, device_id=row_peer(i))
     for s in range(3):
+        loads[s].wait()
         for a in range(32):
             rows[s, 8 * a : 8 * a + 8, :] = raw[s, :, 128 * a : 128 * a + 128]
-    for s in range(3):
-        for ch in range(8):
-            mine[ch, s] = rows[s, pl.ds(ch, 32, stride=8), :]
+        for c in range(HALF):
+            mine[c, s] = rows[s, pl.ds(HALF * (1 - h) + c, 32, stride=8), :]
 
     def way(c, i):
         return 4 + 8 * ((c + i) & 1)
 
     def z1(c, i):
         return pltpu.make_async_remote_copy(
-            mine.at[HALF * (1 - h) + c, i], passing.at[c, i], z1s.at[c, i], pr.at[c, i], device_id=along_z(way(c, i))
+            mine.at[c, i], passing.at[c, i], z1s.at[c, i], pr.at[c, i], device_id=along_z(way(c, i))
         )
 
     def z1_on(c, i):
@@ -120,7 +121,7 @@
 
     def z2(c, i):
         return pltpu.make_async_remote_copy(
-            yout.at[c, 1 - h, i], yrecv.at[c, i], z2s.at[c, i], z2r.at[c, i], device_id=partner
+            ybuf.at[c, 1 - h, i], yrecv.at[c, i], z2s.at[c, i], z2r.at[c, i], device_id=partner
         )
 
     def member(q, side):
@@ -155,17 +156,20 @@
         part = bsend.at[slot, pl.ds(0, PLANE - 1)]
         return pltpu.make_async_remote_copy(part, part, bs.at[slot], br.at[0], device_id=partner)
 
-    pl.semaphore_wait(barrier, PLANE + 1)
+    pl.semaphore_wait(barrier, 8)
 
     @pl.loop(0, HALF)
     def _(c):
         for i in range(Z1_CUT):
             z1(c, i).start()
 
-    @pl.loop(0, HALF)
-    def _(c):
-        vin[c, h] = mine[HALF * h + c]
-
+    for i in range(1, 4):
+        pl.semaphore_signal(ready, 1, device_id=row_peer(i))
+    for copy in loads[3:]:
+        copy.start()
+    for s in range(3):
+        for c in range(HALF):
+            vin[c, h, s] = rows[s, pl.ds(HALF * h + c, 32, stride=8), :]
     for copy in loads[3:]:
         copy.wait()
 
@@ -174,6 +178,8 @@
         for i in range(Z1_CUT):
             z1(c, i).wait_recv()
             z1_on(c, i).start()
+
+    pl.semaphore_wait(ready, 3)
 
     def forward(c):
         for i in range(Z1_CUT):
@@ -248,19 +254,19 @@
         y = mm(inv2[...], tripled(jnp.concatenate(turned, axis=1), 0))
         for out in range(2):
             for half in range(2):
-                yout[c, half, out] = y[32 * half : 32 * (half + 1), B * out : B * (out + 1)]
+                ybuf[c, half, out] = y[32 * half : 32 * (half + 1), B * out : B * (out + 1)]
         for i in range(2):
             z2(c, i).start()
 
+    @pl.loop(0, HALF)
+    def _(c):
+        forward(c)
+
     @pl.loop(0, HALF + I_LAG)
     def _(step):
-        @pl.when(step < HALF)
-        def _():
-            forward(step)
-
-        @pl.when((step >= M_LAG) & (step < HALF + M_LAG) & (((step + M_LAG) & 1) == group))
-        def _():
-            middle(step - M_LAG)
+        @pl.when((step < HALF) & ((step & 1) == group))
+        def _():
+            middle(step)
 
         @pl.when(step >= I_LAG)
         def _():
@@ -281,46 +287,52 @@
         def _():
             fwd_all(c, GROUP).wait_send()
 
-        for out in range(2):
-            orow[out, pl.ds(HALF * h + c, 32, stride=8), :] = yout[c, h, out]
+    own = [pltpu.make_async_copy(ybuf.at[c, h], yout.at[c], in_sem.at[c]) for c in range(HALF)]
+    for copy in own:
+        copy.start()
+    for copy in own:
+        copy.wait()
 
     @pl.loop(0, HALF)
     def _(c):
         for i in range(2):
-            z2(c, i).wait_recv()
-            orow[i, pl.ds(HALF * (1 - h) + c, 32, stride=8), :] = yrecv[c, i]
-
-    for a in range(32):
-        dx_ref[:, 128 * a : 128 * a + 128] = orow[0, 8 * a : 8 * a + 8, :]
-        dr_ref[:, 128 * a : 128 * a + 128] = orow[1, 8 * a : 8 * a + 8, :]
-
-    @pl.loop(0, HALF)
-    def _(c):
-        for i in range(2):
-            z2(c, i).wait_send()
+            z2(c, i).wait()
+
+
+def arrange(own_hbm, other_hbm, dx_ref, dr_ref, own, other, sem):
+    h = lax.axis_index("context") & 1
+    copies = [pltpu.make_async_copy(own_hbm, own, sem.at[0]), pltpu.make_async_copy(other_hbm, other, sem.at[1])]
+    for copy in copies:
+        copy.start()
+    for copy in copies:
+        copy.wait()
+    for out, ref in enumerate((dx_ref, dr_ref)):
+        low = [jnp.where(h == 0, own[c, out], other[c, out]) for c in range(HALF)]
+        high = [jnp.where(h == 0, other[c, out], own[c, out]) for c in range(HALF)]
+        turned = jnp.stack(low + high, axis=1)
+        for a in range(32):
+            ref[:, 128 * a : 128 * a + 128] = turned[a]
 
 
 def per_device(inputs, grads, response):
     consts = tables()
     f32, bf16 = jnp.float32, jnp.bfloat16
     vmem, dma = pltpu.VMEM, pltpu.SemaphoreType.DMA
-    return pl.pallas_call(
+    own, other = pl.pallas_call(
         kernel,
-        out_shape=(jax.ShapeDtypeStruct(inputs.shape, f32),) * 2,
+        out_shape=(jax.ShapeDtypeStruct((HALF, 2, 32, B), f32),) * 2,
         in_specs=[pl.BlockSpec(memory_space=pl.ANY)] * 8,
-        out_specs=(pl.BlockSpec(memory_space=vmem),) * 2,
+        out_specs=(pl.BlockSpec(memory_space=pl.ANY),) * 2,
         scratch_shapes=[
             vmem((3, 8, 4096), f32),
             vmem((3, 256, 128), f32),
-            vmem((8, Z1_CUT, 32, 128), f32),
+            vmem((HALF, Z1_CUT, 32, 128), f32),
             vmem((HALF, 2, Z1_CUT, 32, 128), f32),
             vmem((HALF, GROUP, 3, 8, 2 * B), f32),
             vmem((2, PLANE, 3, 8, 2 * B), f32),
             vmem((2, PLANE, 2, 8, 2 * B), f32),
             vmem((HALF, GROUP, 2, 8, 2 * B), f32),
             vmem((HALF, 2, 2, 32, 128), f32),
-            vmem((HALF, 2, 32, 128), f32),
-            vmem((2, 256, 128), f32),
             vmem((2 * A, 3 * A), bf16),
             vmem((6 * B, 2 * B), bf16),
             vmem((6 * B, 2 * B), bf16),
@@ -333,10 +345,19 @@
             dma((HALF,)), dma((2,)),
             dma((2,)), dma((HALF,)),
             dma((HALF, 2)), dma((HALF, 2)),
+            pltpu.SemaphoreType.REGULAR,
         ],
         compiler_params=pltpu.CompilerParams(collective_id=0, has_side_effects=True),
         name="hyena_backward",
     )(inputs, grads, response, *(jnp.asarray(t) for t in consts))
+    return pl.pallas_call(
+        arrange,
+        out_shape=(jax.ShapeDtypeStruct(inputs.shape, f32),) * 2,
+        in_specs=[pl.BlockSpec(memory_space=pl.ANY)] * 2,
+        out_specs=(pl.BlockSpec(memory_space=vmem),) * 2,
+        scratch_shapes=[vmem((HALF, 2, 32, B), f32), vmem((HALF, 2, 32, B), f32), dma((2,))],
+        name="arrange",
+    )(own, other)
 
 
 def solution(mesh):

time: 66.1 us -> 63.7 us (0.964)
  the two profiles are of different devices: /device:TPU:8 before, /device:TPU:100 now
where the time goes in v4:
time: 63.7 us; the launch traced here: 63.6 us
  Pallas kernels  62.9 us (99%)
  between operations  0.64 us (1%)
    pallas_call x1, Pallas kernels, per_device(): pl.pallas_call(kernel, out_shape=(jax.ShapeDtypeStruct((HALF, 2, 32, B),...  61 us
    pallas_call x1, Pallas kernels, per_device(): pl.pallas_call(arrange, out_shape=(jax.ShapeDtypeStruct(inputs.shape, f32...  1.88 us

profile of v4, /device:TPU:100, one launch (start us, length us, event | category | flops | bytes accessed | tf_op | source)
XLA Modules:
  0.0 63.6 jit_solution(3308189566289676347)
XLA Ops:
  0.6 61.0 %hyena_backward.1 = (f32[4,2,32,128]{3,2,1,0:T(8,128)}, f32[4,2,32,128]{3,2,1,0:T(8,128)}) custom-call(f32[8,4096]{1,0:T(8,128)} %x_hbm.1, f32[8,4096]{1,0:T(8,128)} %g_hbm.1, f32[8,4096]{1,0:T(8,128)} %r_hbm.1, bf16[128,192]{1,0:T(8,128)(2,1)} %constant.10.clone.fwd1_hbm, bf16[768,256]{1,0:T(8,128)(2,1)} %constant.11.clone.fwd2_hbm, ...), custom_call_target="tpu_custom_call" | custom-call | tf_op jit(solution)/shard_map/hyena_backward/pallas_call | solution.py:321
  61.7 1.9 %arrange.1 = (f32[8,4096]{1,0:T(8,128)}, f32[8,4096]{1,0:T(8,128)}) custom-call(f32[4,2,32,128]{3,2,1,0:T(8,128)} %get-tuple-element.4.own_hbm, f32[4,2,32,128]{3,2,1,0:T(8,128)} %get-tuple-element.5.other_hbm), custom_call_target="tpu_custom_call" | custom-call | tf_op jit(solution)/shard_map/arrange/pallas_call | solution.py:353

commit v5 on v4

--- a/solution.py
+++ b/solution.py
@@ -14,7 +14,7 @@
 A, B = 64, 128
 BLOCK = A * B
 Z1_CUT = 3
-I_LAG = 2
+I_LAG = 3
 
 
 def split_bf16(table):
@@ -231,8 +231,11 @@
                     total_im = add_im if total_im is None else total_im + add_im
                 bsend[slot, k, out, :, :B] = total_re
                 bsend[slot, k, out, :, B:] = total_im
-        for i in range(1, PLANE):
-            back(c, (m + i) & 15).start()
+
+            @pl.when(m != k)
+            def _(k=k):
+                back(c, k).start()
+
         brecv[c, place] = bsend[slot, m]
 
     def inverse(c):

time: 63.7 us -> 63.1 us (level)
  the two profiles are of different devices: /device:TPU:100 before, /device:TPU:22 now
where the time goes in v5:
time: 63.1 us; the launch traced here: 62.9 us
  Pallas kernels  62.3 us (99%)
  between operations  0.64 us (1%)
    pallas_call x1, Pallas kernels, per_device(): pl.pallas_call(kernel, out_shape=(jax.ShapeDtypeStruct((HALF, 2, 32, B),...  60.4 us
    pallas_call x1, Pallas kernels, per_device(): pl.pallas_call(arrange, out_shape=(jax.ShapeDtypeStruct(inputs.shape, f32...  1.88 us

profile of v5, /device:TPU:22, one launch (start us, length us, event | category | flops | bytes accessed | tf_op | source)
XLA Modules:
  0.0 62.9 jit_solution(5744752854632946563)
XLA Ops:
  0.6 60.4 %hyena_backward.1 = (f32[4,2,32,128]{3,2,1,0:T(8,128)}, f32[4,2,32,128]{3,2,1,0:T(8,128)}) custom-call(f32[8,4096]{1,0:T(8,128)} %x_hbm.1, f32[8,4096]{1,0:T(8,128)} %g_hbm.1, f32[8,4096]{1,0:T(8,128)} %r_hbm.1, bf16[128,192]{1,0:T(8,128)(2,1)} %constant.10.clone.fwd1_hbm, bf16[768,256]{1,0:T(8,128)(2,1)} %constant.11.clone.fwd2_hbm, ...), custom_call_target="tpu_custom_call" | custom-call | tf_op jit(solution)/shard_map/hyena_backward/pallas_call | solution.py:324
  61.0 1.9 %arrange.1 = (f32[8,4096]{1,0:T(8,128)}, f32[8,4096]{1,0:T(8,128)}) custom-call(f32[4,2,32,128]{3,2,1,0:T(8,128)} %get-tuple-element.4.own_hbm, f32[4,2,32,128]{3,2,1,0:T(8,128)} %get-tuple-element.5.other_hbm), custom_call_target="tpu_custom_call" | custom-call | tf_op jit(solution)/shard_map/arrange/pallas_call | solution.py:356

commit v6 on v5

--- a/solution.py
+++ b/solution.py
@@ -119,9 +119,9 @@
             passing.at[c, i], vin.at[c, 1 - h, i], ps.at[c, i], z1r.at[c, i], device_id=along_z(way(c, i))
         )
 
-    def z2(c, i):
-        return pltpu.make_async_remote_copy(
-            ybuf.at[c, 1 - h, i], yrecv.at[c, i], z2s.at[c, i], z2r.at[c, i], device_id=partner
+    def z2(c):
+        return pltpu.make_async_remote_copy(
+            ybuf.at[c, 1 - h], yrecv.at[c], z2s.at[c], z2r.at[c], device_id=partner
         )
 
     def member(q, side):
@@ -258,8 +258,7 @@
         for out in range(2):
             for half in range(2):
                 ybuf[c, half, out] = y[32 * half : 32 * (half + 1), B * out : B * (out + 1)]
-        for i in range(2):
-            z2(c, i).start()
+        z2(c).start()
 
     @pl.loop(0, HALF)
     def _(c):
@@ -298,8 +297,7 @@
 
     @pl.loop(0, HALF)
     def _(c):
-        for i in range(2):
-            z2(c, i).wait()
+        z2(c).wait()
 
 
 def arrange(own_hbm, other_hbm, dx_ref, dr_ref, own, other, sem):
@@ -347,7 +345,7 @@
             dma((HALF, Z1_CUT)), dma((HALF, Z1_CUT)),
             dma((HALF,)), dma((2,)),
             dma((2,)), dma((HALF,)),
-            dma((HALF, 2)), dma((HALF, 2)),
+            dma((HALF,)), dma((HALF,)),
             pltpu.SemaphoreType.REGULAR,
         ],
         compiler_params=pltpu.CompilerParams(collective_id=0, has_side_effects=True),

time: 63.1 us -> 63 us (level)
  no operation moved by 1% of the time
where the time goes in v6:
time: 63 us; the launch traced here: 62.8 us
  Pallas kernels  62.2 us (99%)
  between operations  0.64 us (1%)
    pallas_call x1, Pallas kernels, per_device(): pl.pallas_call(kernel, out_shape=(jax.ShapeDtypeStruct((HALF, 2, 32, B),...  60.3 us
    pallas_call x1, Pallas kernels, per_device(): pl.pallas_call(arrange, out_shape=(jax.ShapeDtypeStruct(inputs.shape, f32...  1.88 us

profile of v6, /device:TPU:22, one launch (start us, length us, event | category | flops | bytes accessed | tf_op | source)
XLA Modules:
  0.0 62.8 jit_solution(8921859941534977981)
XLA Ops:
  0.6 60.3 %hyena_backward.1 = (f32[4,2,32,128]{3,2,1,0:T(8,128)}, f32[4,2,32,128]{3,2,1,0:T(8,128)}) custom-call(f32[8,4096]{1,0:T(8,128)} %x_hbm.1, f32[8,4096]{1,0:T(8,128)} %g_hbm.1, f32[8,4096]{1,0:T(8,128)} %r_hbm.1, bf16[128,192]{1,0:T(8,128)(2,1)} %constant.10.clone.fwd1_hbm, bf16[768,256]{1,0:T(8,128)(2,1)} %constant.11.clone.fwd2_hbm, ...), custom_call_target="tpu_custom_call" | custom-call | tf_op jit(solution)/shard_map/hyena_backward/pallas_call | solution.py:322
  61.0 1.9 %arrange.1 = (f32[8,4096]{1,0:T(8,128)}, f32[8,4096]{1,0:T(8,128)}) custom-call(f32[4,2,32,128]{3,2,1,0:T(8,128)} %get-tuple-element.4.own_hbm, f32[4,2,32,128]{3,2,1,0:T(8,128)} %get-tuple-element.5.other_hbm), custom_call_target="tpu_custom_call" | custom-call | tf_op jit(solution)/shard_map/arrange/pallas_call | solution.py:354
